TPU v7x, 32 devices: a whole 2x2x4 slice. The times are simulated.
32 devices in a mesh: parts: 2 (over y), tensor: 4 (over z), dp: 4 (over x, core).
Axes of the slice: x: 2, y: 2, z: 4, core: 2. Of those that a mesh axis runs over, the one named last changes fastest.
Arguments:
- inputs: bfloat16 [4096, 8192], P(('parts', 'dp'), 'tensor'), parts along dimension 0, may hold values from -6 to 6
- cotangent: bfloat16 [4096, 8192], P(('parts', 'dp'), 'tensor'), parts along dimension 0, may hold values from -6 to 6
- weight: bfloat16 [8192, 8192], P(None, 'tensor'), may hold values from -0.0625 to 0.0625
- down_weight_maps: bfloat16 [8192, 2048], P('tensor', 'parts'), parts along dimension 1, may hold values from -0.0625 to 0.0625
- up_weight_maps: bfloat16 [2048, 8192], P('parts', 'tensor'), parts along dimension 0, may hold values from -0.75 to 0.75
- counts: int32 [8, 16], P('parts'), parts along dimension 0, may hold values from 0 to 256, as said below
- ranks: int32 [32], P('parts'), parts along dimension 0, may hold values from 8 to 64, as said below
- owners: int32 [32], P('parts'), parts along dimension 0, may hold values from 0 to 3
Outputs:
- projected: bfloat16 [4096, 8192], P(('parts', 'dp'), 'tensor'), parts along dimension 0
- input_grad: bfloat16 [4096, 8192], P(('parts', 'dp'), 'tensor'), parts along dimension 0
- grad_a: float32 [8, 8192, 1024], P(('parts', 'dp'), 'tensor'), parts along dimension 0
- grad_b: float32 [8, 1024, 8192], P(('parts', 'dp'), None, 'tensor'), parts along dimension 0
There are 2 independent parts, one for each index of `parts`. A program takes and returns all parts, laid end to end along the dimension named above; an argument that names none is the same for every part. Nothing has to cross between parts.
Inputs may be any that keep to these rules, and one draw needn't show every extreme that they name: `counts`: each row sums to at most 512, one row to exactly 512, and all rows together to exactly 1024; some entry is exactly 256. `ranks`: each rank is 64 divided by 1, 2, 4 or 8; some trial has 64 and some 64 // 8.
All inputs are finite; a program needn't handle non-finite values.
Results may differ from a plain program's by a relative error of at most 0.0034.
Values may be sent and summed in bfloat16 or wider, within the bound.
A program may use at most 256 MiB of HBM per device.

v0:
```python
import jax
import jax.numpy as jnp
from jax import lax
from jax.sharding import PartitionSpec as P

LARGEST_RANK = 64
TRIALS = 16


adapter_alpha = 16.0


def local(inputs, cotangent, weight, down_weight_maps, up_weight_maps, counts, ranks, owners):
    slot_count, feature_local = inputs.shape
    group_count = counts.shape[0]
    adapter_rank_width = down_weight_maps.shape[1]
    column = jnp.arange(adapter_rank_width, dtype=jnp.int32)
    col_trial = column // LARGEST_RANK
    column_slot = column % LARGEST_RANK
    trial_ids = jnp.arange(TRIALS, dtype=jnp.int32)
    matches = col_trial[:, None] == trial_ids[None, :]
    rank_per_column = jnp.sum(jnp.where(matches, ranks[None, :], 0), axis=1)
    owner_col = jnp.sum(jnp.where(matches, owners[None, :], 0), axis=1)
    scale_per_column = jnp.where(
        column_slot < rank_per_column, adapter_alpha / rank_per_column.astype(jnp.float32), 0.0
    )
    trial_rows = jnp.sum(counts, axis=0)
    per_trial = 1.0 / jnp.maximum(trial_rows, 1).astype(jnp.float32)
    inverse_col = jnp.sum(jnp.where(matches, per_trial[None, :], 0.0), axis=1)
    cumulative = jnp.cumsum(counts, axis=1)
    group_ids = jnp.arange(group_count, dtype=jnp.int32)
    my_group = lax.axis_index("dp")
    contract_trailing = (((1,), (1,)), ((), ()))
    contract_first = (((0,), (0,)), ((), ()))
    positions = jnp.arange(slot_count, dtype=jnp.int32)
    my_bounds = jnp.sum(jnp.where((group_ids == my_group)[:, None], cumulative, 0), axis=0)
    row_trial = jnp.sum((positions[:, None] >= my_bounds[None, :]).astype(jnp.int32), axis=1)
    is_live = row_trial < TRIALS
    coef = jnp.where(row_trial[:, None] == col_trial[None, :], scale_per_column[None, :], 0.0)
    frozen_output = jnp.dot(
        lax.all_gather(inputs, "tensor", axis=1, tiled=True),
        weight,
        preferred_element_type=jnp.float32,
    )
    down_projected_sum = lax.psum(
        jnp.dot(inputs, down_weight_maps, preferred_element_type=jnp.float32), "tensor"
    )
    scaled_down_projected = (coef * down_projected_sum).astype(jnp.bfloat16)
    merged_output = frozen_output + jnp.dot(
        scaled_down_projected, up_weight_maps, preferred_element_type=jnp.float32
    )
    result = jnp.where(is_live[:, None], merged_output, 0.0).astype(jnp.bfloat16)
    back_part = lax.dot_general(
        cotangent, up_weight_maps, contract_trailing, preferred_element_type=jnp.float32
    )
    back_sum = lax.psum(back_part, "tensor")
    scaled_up_projected = (coef * back_sum).astype(jnp.bfloat16)
    frozen_back = lax.dot_general(
        cotangent, weight, contract_trailing, preferred_element_type=jnp.float32
    )
    frozen_share = lax.psum_scatter(frozen_back, "tensor", scatter_dimension=1, tiled=True)
    adapter_in = lax.dot_general(
        scaled_up_projected, down_weight_maps, contract_trailing, preferred_element_type=jnp.float32
    )
    gradient = jnp.where(is_live[:, None], frozen_share + adapter_in, 0.0).astype(jnp.bfloat16)
    term_a = (
        lax.dot_general(
            inputs, scaled_up_projected, contract_first, preferred_element_type=jnp.float32
        )
        * inverse_col[None, :]
    )
    term_b = (
        lax.dot_general(
            scaled_down_projected, cotangent, contract_first, preferred_element_type=jnp.float32
        )
        * inverse_col[:, None]
    )
    projected, input_grad, term_a, term_b = (result, gradient, term_a, term_b)
    full_a, full_b = lax.psum((term_a, term_b), "dp")
    owned_mine = (owner_col == my_group).astype(jnp.float32)
    grad_a = (full_a * owned_mine[None, :])[None]
    grad_b = (full_b * owned_mine[:, None])[None]
    return (projected, input_grad, grad_a, grad_b)


def solution(mesh):
    return jax.shard_map(
        local,
        mesh=mesh,
        in_specs=(
            P(("parts", "dp"), "tensor"),
            P(("parts", "dp"), "tensor"),
            P(None, "tensor"),
            P("tensor", "parts"),
            P("parts", "tensor"),
            P("parts", None),
            P("parts"),
            P("parts"),
        ),
        out_specs=(
            P(("parts", "dp"), "tensor"),
            P(("parts", "dp"), "tensor"),
            P(("parts", "dp"), "tensor", None),
            P(("parts", "dp"), None, "tensor"),
        ),
        check_vma=False,
    )
```

profile of v0, /device:TPU:0, one launch (start us, length us, event | category | flops | bytes accessed | tf_op | source)
XLA Modules:
  0.0 924.6 jit_solution(6488323135650758244)
XLA Ops:
  7.2 0.0 copy-start
  7.2 0.0 all-reduce.7.cloned.1.call-start
  7.2 0.0 copy-start.7
  7.2 6.6 fusion.15
  13.9 0.0 copy-done
  13.9 0.0 copy-done.7
  13.9 3.7 fusion.17
  17.5 0.0 copy-start.4
  17.6 0.0 copy-start.5
  17.6 0.0 copy-start.6
  17.6 0.0 all-reduce.7.cloned.1.call-update
  17.6 0.0 all-reduce.5.cloned.1.call-start
  17.6 0.6 copy-done.4
  18.2 0.2 reduce_window_sum.11
  18.5 0.1 select_reduce_fusion.3
  18.5 0.1 convert_reduce_fusion
  18.6 0.1 select_reduce_fusion.1
  18.7 0.0 copy-done.5
  18.7 0.0 copy-done.6
  18.8 0.1 select_reduce_fusion
  18.9 156.9 %all-reduce.7.cloned.1.call-done = (f32[512,1024]{1,0:T(8,128)}, f32[512,1024]{1,0:T(8,128)}) async-done(((f32[512,1024]{1,0:T(8,128)}, f32[512,1024]{1,0:T(8,128)}), (f32[512,1024]{1,0:T(8,128)}, f32[512,1024]{1,0:T(8,128)})) %all-reduce.7.cloned.1.call-update) | async-done | bytes 4194320 | tf_op jit(solution)/shard_map/psum | solution.py:45
  175.8 0.0 copy-start.2
  175.8 8.2 multiply_bitcast_fusion.2
  184.0 0.0 copy-done.2
  184.0 5.9 convolution_multiply_fusion
  189.9 0.0 all-reduce.5.cloned.1.call-update
  190.0 0.0 all-gather.2.cloned.1.call-start
  190.0 0.7 all-gather.2.cloned.1.call-update
  190.7 0.2 reduce-scatter.2.cloned.1.call-start
  190.9 25.8 %fusion.16 = f32[512,8192]{1,0:T(8,128)} fusion(bf16[512,2048]{1,0:T(8,128)(2,1)S(1)} %copy-done, bf16[8192,2048]{1,0:T(8,128)(2,1)} %param.10), kind=kOutput, calls=%fused_computation.36 | convolution fusion | flops 17179869184 | bytes 52428800 | tf_op jit(solution)/shard_map/dot_general | solution.py:58
  216.7 0.0 copy-start.3
  216.7 0.0 reduce-scatter.2.cloned.1.call-update
  216.8 1.6 copy-done.3
  218.4 6.5 fusion.13
  224.9 253.1 %all-reduce.5.cloned.1.call-done = (f32[2048,1024]{0,1:T(8,128)}, f32[1024,2048]{1,0:T(8,128)}) async-done(((f32[2048,1024]{0,1:T(8,128)}, f32[1024,2048]{1,0:T(8,128)}), (f32[2048,1024]{0,1:T(8,128)}, f32[1024,2048]{1,0:T(8,128)})) %all-reduce.5.cloned.1.call-update) | async-done | bytes 16777232 | tf_op jit(solution)/shard_map/psum | solution.py:79
  478.0 7.4 multiply_bitcast_fusion.1
  485.3 9.7 %copy.13 = f32[1,2048,1024]{2,1,0:T(8,128)} copy(f32[1,2048,1024]{1,2,0:T(8,128)} %multiply_bitcast_fusion.1) | data formatting | bytes 16777216
  495.1 7.4 multiply_bitcast_fusion
  502.5 126.8 %all-gather.2.cloned.1.call-done = bf16[512,8192]{1,0:T(8,128)(2,1)} async-done(((bf16[512,2048]{1,0:T(8,128)(2,1)}), bf16[512,8192]{1,0:T(8,128)(2,1)}) %all-gather.2.cloned.1.call-update) | async-done | bytes 8388624 | tf_op jit(solution)/shard_map/all_gather | solution.py:41
  629.3 24.9 %select_convert_fusion.1 = bf16[512,2048]{1,0:T(8,128)(2,1)} fusion(f32[512,2048]{1,0:T(8,128)} %fusion.13, bf16[512,8192]{1,0:T(8,128)(2,1)} %all-gather.2.cloned.1.call-done, bf16[8192,2048]{1,0:T(8,128)(2,1)} %param.10, pred[512]{0:T(512)(128)(4,1)S(1)} %broadcast_compare_fusion), kind=kOutput, calls=%fused_computation.5 | convolution fusion | flops 17183014912 | bytes 48235008 | tf_op jit(solution)/shard_map/dot_general | solution.py:40
  654.2 255.9 %reduce-scatter.2.cloned.1.call-done = f32[512,2048]{1,0:T(8,128)} async-done(((f32[512,8192]{1,0:T(8,128)}), f32[512,2048]{1,0:T(8,128)}) %reduce-scatter.2.cloned.1.call-update) | async-done | bytes 4194320 | tf_op jit(solution)/shard_map/reduce_scatter | solution.py:61
  910.1 0.0 copy-start.1
  910.1 7.9 select_convert_fusion
  918.1 0.0 copy-done.1
  (7 shorter events, 0.1 us)
Async XLA Ops:
  7.2 6.7 copy-start
  7.2 168.6 %all-reduce.7.cloned.1.call-start = ((), (), s32[]{:S(2)}) async-start(), calls=%async_computation.4 | async-start | bytes 8388608 | tf_op jit(solution)/shard_map/psum | solution.py:45
  7.2 6.6 copy-start.7
  17.5 0.7 copy-start.4
  17.6 1.2 copy-start.5
  17.6 1.2 copy-start.6
  17.6 460.4 %all-reduce.5.cloned.1.call-start = ((), (), s32[]{:S(2)}) async-start(), calls=%async_computation.3 | async-start | bytes 33554432 | tf_op jit(solution)/shard_map/psum | solution.py:79
  175.8 8.3 copy-start.2
  190.0 439.3 %all-gather.2.cloned.1.call-start = ((), (), s32[]{:S(2)}) async-start(), calls=%async_computation.1 | async-start | bytes 10485760 | tf_op jit(solution)/shard_map/all_gather | solution.py:41
  190.7 719.4 %reduce-scatter.2.cloned.1.call-start = ((), (), s32[]{:S(2)}) async-start(), calls=%async_computation.2 | async-start | bytes 20971520 | tf_op jit(solution)/shard_map/reduce_scatter | solution.py:61
  216.7 1.7 copy-start.3
  910.1 7.9 copy-start.1
Sparse Core Ops, SparseCore 0:
  17.7 158.0 all-reduce.6
  190.1 287.8 all-reduce.4
  479.6 149.6 all-gather.1
  631.6 278.4 reduce-scatter.1
where the time goes:
time: 925 us
  waiting for transfers between devices  793 us (86%)
  matrix products  89.6 us (10%)
  other arithmetic  15.4 us (2%)
  between operations  13.9 us (2%)
  local copies, waits for them, and re-layouts  12 us (1%)
    reduce_scatter x1, waiting for transfers between devices, local(): lax.psum_scatter(frozen_back, 'tensor', scatter_dimension=1, tiled=True)  256 us
    psum x1, waiting for transfers between devices, local(): full_a, full_b = lax.psum((term_a, term_b), 'dp')  253 us
    psum x1, waiting for transfers between devices, local(): lax.psum(jnp.dot(inputs, down_weight_maps, preferred_element_type=jnp.flo...  157 us
    all_gather x1, waiting for transfers between devices, local(): lax.all_gather(inputs, 'tensor', axis=1, tiled=True)  127 us
    dot_general x1, matrix products, local(): lax.dot_general(cotangent, weight, contract_trailing, preferred_element_t...  25.8 us
    dot_general x1, matrix products, local(): jnp.dot(lax.all_gather(inputs, 'tensor', axis=1, tiled=True), weight, pre...  24.9 us
  transfers between devices with their start and end apart: 4, of which 4 were waited for; matrix products, arithmetic and copies ran while one was open for 9% of the time, Pallas kernels for 0%

commit v1 on v0

v1 whole, which is shorter than its diff:
```python
import jax
import jax.numpy as jnp
from jax import lax
from jax.sharding import PartitionSpec as P

LARGEST_RANK = 64
TRIALS = 16
LANES = 128

adapter_alpha = 16.0

TRAILING = (((1,), (1,)), ((), ()))
FIRST = (((0,), (0,)), ((), ()))


def fold_columns(values, match):
    width = values.shape[1]
    kept = jnp.where(match, values, 0.0)
    return sum(kept[:, i : i + LANES] for i in range(0, width, LANES))


def spread_columns(folded, match):
    repeats = match.shape[1] // LANES
    return jnp.where(match, jnp.concatenate([folded] * repeats, axis=1), jnp.zeros((), folded.dtype))


def local(inputs, cotangent, weight, down_weight_maps, up_weight_maps, counts, ranks, owners):
    slot_count, feature_local = inputs.shape
    group_count = counts.shape[0]
    width = down_weight_maps.shape[1]
    column = jnp.arange(width, dtype=jnp.int32)
    col_trial = column // LARGEST_RANK
    column_slot = column % LARGEST_RANK
    trial_ids = jnp.arange(TRIALS, dtype=jnp.int32)
    matches = col_trial[:, None] == trial_ids[None, :]
    rank_per_column = jnp.sum(jnp.where(matches, ranks[None, :], 0), axis=1)
    owner_col = jnp.sum(jnp.where(matches, owners[None, :], 0), axis=1)
    scale_per_column = jnp.where(
        column_slot < rank_per_column, adapter_alpha / rank_per_column.astype(jnp.float32), 0.0
    )
    trial_rows = jnp.sum(counts, axis=0)
    per_trial = 1.0 / jnp.maximum(trial_rows, 1).astype(jnp.float32)
    inverse_col = jnp.sum(jnp.where(matches, per_trial[None, :], 0.0), axis=1)
    cumulative = jnp.cumsum(counts, axis=1)
    group_ids = jnp.arange(group_count, dtype=jnp.int32)
    my_group = lax.axis_index("dp")
    positions = jnp.arange(slot_count, dtype=jnp.int32)
    trial_all = jnp.sum(
        (positions[None, :, None] >= cumulative[:, None, :]).astype(jnp.int32), axis=2
    )
    row_trial = jnp.sum(jnp.where((group_ids == my_group)[:, None], trial_all, 0), axis=0)
    is_live = row_trial < TRIALS
    match = row_trial[:, None] == col_trial[None, :]
    match_all = trial_all.reshape(-1)[:, None] == col_trial[None, :]
    coef = jnp.where(match, scale_per_column[None, :], 0.0)
    coef_folded = fold_columns(coef, match)

    down_part = jnp.dot(inputs, down_weight_maps, preferred_element_type=jnp.float32)
    back_part = lax.dot_general(
        cotangent, up_weight_maps, TRAILING, preferred_element_type=jnp.float32
    )
    folded = jnp.concatenate([fold_columns(down_part, match), fold_columns(back_part, match)], axis=1)
    folded = lax.psum(folded, "tensor")
    scaled_down_f = (coef_folded * folded[:, :LANES]).astype(jnp.bfloat16)
    scaled_back_f = (coef_folded * folded[:, LANES:]).astype(jnp.bfloat16)

    all_inputs = lax.all_gather(inputs, "tensor", axis=1, tiled=True)
    mine = lax.axis_index("tensor")
    block = jnp.arange(weight.shape[0], dtype=jnp.int32) // feature_local
    frozen_back = lax.dot_general(cotangent, weight, TRAILING, preferred_element_type=jnp.float32)
    others = jnp.where((block == mine)[None, :], 0.0, frozen_back).astype(jnp.bfloat16)
    others_share = lax.psum_scatter(others, "tensor", scatter_dimension=1, tiled=True)
    own_weight = lax.dynamic_slice_in_dim(weight, mine * feature_local, feature_local, 0)
    own_share = lax.dot_general(cotangent, own_weight, TRAILING, preferred_element_type=jnp.float32)
    frozen_share = own_share + others_share.astype(jnp.float32)

    group_inputs = lax.all_gather(inputs, "dp", axis=0, tiled=True)
    group_cotangent = lax.all_gather(cotangent, "dp", axis=0, tiled=True)
    both = lax.all_gather(
        jnp.concatenate([scaled_down_f, scaled_back_f], axis=1), "dp", axis=0, tiled=True
    )

    frozen_output = jnp.dot(all_inputs, weight, preferred_element_type=jnp.float32)
    scaled_down = spread_columns(scaled_down_f, match)
    scaled_back = spread_columns(scaled_back_f, match)
    merged = frozen_output + jnp.dot(scaled_down, up_weight_maps, preferred_element_type=jnp.float32)
    projected = jnp.where(is_live[:, None], merged, 0.0).astype(jnp.bfloat16)
    adapter_in = lax.dot_general(
        scaled_back, down_weight_maps, TRAILING, preferred_element_type=jnp.float32
    )
    input_grad = jnp.where(
        is_live[:, None], frozen_share + adapter_in, 0.0
    ).astype(jnp.bfloat16)

    owned = jnp.where(owner_col == my_group, inverse_col, 0.0)
    down_all = spread_columns(both[:, :LANES], match_all)
    back_all = spread_columns(both[:, LANES:], match_all)
    grad_a = lax.dot_general(group_inputs, back_all, FIRST, preferred_element_type=jnp.float32)
    grad_b = lax.dot_general(down_all, group_cotangent, FIRST, preferred_element_type=jnp.float32)
    grad_a = (grad_a * owned[None, :])[None]
    grad_b = (grad_b * owned[:, None])[None]
    return (projected, input_grad, grad_a, grad_b)


def solution(mesh):
    return jax.shard_map(
        local,
        mesh=mesh,
        in_specs=(
            P(("parts", "dp"), "tensor"),
            P(("parts", "dp"), "tensor"),
            P(None, "tensor"),
            P("tensor", "parts"),
            P("parts", "tensor"),
            P("parts", None),
            P("parts"),
            P("parts"),
        ),
        out_specs=(
            P(("parts", "dp"), "tensor"),
            P(("parts", "dp"), "tensor"),
            P(("parts", "dp"), "tensor", None),
            P(("parts", "dp"), None, "tensor"),
        ),
        check_vma=False,
    )
```

time: 925 us -> 512 us (0.55)
  waiting for transfers between devices: 793 us -> 354 us
  matrix products: 89.6 us -> 109 us
  local copies, waits for them, and re-layouts: 12 us -> 27.7 us
    psum x2 -> x1, waiting for transfers between devices: 410 us -> 40.7 us  [local(): folded = lax.psum(folded, 'tensor')]
    reduce_scatter x1, waiting for transfers between devices: 256 us -> 120 us  [local(): lax.psum_scatter(others, 'tensor', scatter_dimension=1, tiled=True)]
    all_gather x1 -> x4, waiting for transfers between devices: 127 us -> 191 us  [the longest x1 136 us: local(): all_inputs = lax.all_gather(inputs, 'tensor', axis=1, tiled=True)]
    dot_general x7 -> x8, matrix products: 83 us -> 107 us  [the longest x1 24.9 us: local(): jnp.dot(all_inputs, weight, preferred_element_type=jnp.float32)]
    broadcast_in_dim x2 -> x0, other arithmetic: 14.8 us -> none  [the longest x1 7.39 us: local(): grad_a = (full_a * owned_mine[None, :])[None]]
    unnamed x17 -> x45, local copies, waits for them, and re-layouts: 12 us -> 25.8 us
  transfers between devices with their start and end apart: 4 -> 6, of which waited for: 4 -> 5; matrix products, arithmetic and copies ran while one was open for 9% -> 23% of each run, Pallas kernels for 0% -> 0%
where the time goes in v1:
time: 512 us; the launch traced here: 511 us
  waiting for transfers between devices  354 us (69%)
  matrix products  109 us (21%)
  local copies, waits for them, and re-layouts  27.7 us (5%)
  between operations  14.4 us (3%)
  other arithmetic  6.18 us (1%)
    all_gather x1, waiting for transfers between devices, local(): all_inputs = lax.all_gather(inputs, 'tensor', axis=1, tiled=True)  136 us
    reduce_scatter x1, waiting for transfers between devices, local(): lax.psum_scatter(others, 'tensor', scatter_dimension=1, tiled=True)  120 us
    psum x1, waiting for transfers between devices, local(): folded = lax.psum(folded, 'tensor')  40.7 us
    all_gather x1, waiting for transfers between devices, local(): group_cotangent = lax.all_gather(cotangent, 'dp', axis=0, tiled=True)  35.6 us
    unnamed x45, local copies, waits for them, and re-layouts  25.8 us
    dot_general x1, matrix products, local(): jnp.dot(all_inputs, weight, preferred_element_type=jnp.float32)  24.9 us
    dot_general x1, matrix products, local(): lax.dot_general(cotangent, weight, TRAILING, preferred_element_type=jnp.f...  24.4 us
    all_gather x1, waiting for transfers between devices, local(): group_inputs = lax.all_gather(inputs, 'dp', axis=0, tiled=True)  19.4 us
  transfers between devices with their start and end apart: 6, of which 5 were waited for; matrix products, arithmetic and copies ran while one was open for 23% of the time, Pallas kernels for 0%

profile of v1, /device:TPU:0, one launch (start us, length us, event | category | flops | bytes accessed | tf_op | source)
XLA Modules:
  0.0 511.5 jit_solution(14548352022868119628)
XLA Ops:
  7.2 0.0 all-reduce.2.cloned.1.call-start
  7.2 0.9 reduce_window_sum.11
  8.1 0.1 convert_reduce_fusion
  8.2 0.1 select_reduce_fusion.3
  8.3 5.3 %compare_select_fusion.4 = f32[512,1024]{1,0:T(8,128)S(1)} fusion(bf16[512,2048]{1,0:T(8,128)(2,1)} %param.9, bf16[1024,2048]{1,0:T(8,128)(2,1)} %param.12, s32[1024]{0:T(1024)S(1)} %add_select_fusion.1, s32[512]{0:T(512)S(1)} %select_reduce_fusion.3), kind=kOutput, calls=%fused_computation.9 | convolution fusion | flops 2148532224 | bytes 8394752 | tf_op jit(solution)/shard_map/dot_general | solution.py:59
  13.6 0.1 slice_add_fusion
  13.8 0.0 copy-done.1
  13.8 0.0 copy-done.7
  13.8 0.0 copy-start.5
  13.8 0.0 copy-start.6
  13.8 2.3 compare_select_fusion.5
  16.1 0.1 slice_add_fusion.7
  16.2 0.8 pad_maximum_fusion
  17.1 0.0 all-reduce.2.cloned.1.call-update
  17.1 0.0 all-gather.7.cloned.1.call-start
  17.1 0.0 copy-done.5
  17.2 0.0 copy-done.6
  17.2 0.1 select_reduce_fusion.1
  17.3 0.3 compare_select_fusion.6
  17.6 40.7 %all-reduce.2.cloned.1.call-done = f32[512,256]{1,0:T(8,128)} async-done(((f32[512,256]{1,0:T(8,128)}), f32[512,256]{1,0:T(8,128)}) %all-reduce.2.cloned.1.call-update) | async-done | bytes 524304 | tf_op jit(solution)/shard_map/psum | solution.py:63
  58.2 1.1 constant_dynamic-update-slice_fusion.15
  59.3 0.0 copy-start.2
  59.3 1.8 constant_dynamic-update-slice_fusion.7
  61.1 0.7 pad_maximum_fusion.1
  61.8 0.0 all-gather.7.cloned.1.call-update
  61.8 0.0 all-gather.9.cloned.1.call-start
  61.9 0.7 all-gather.9.cloned.1.call-update
  62.6 0.0 all-gather.11.cloned.1.call-start
  62.6 0.5 all-gather.11.cloned.1.call-update
  63.2 0.0 all-gather.5.cloned.1.call-start
  63.2 0.5 all-gather.5.cloned.1.call-update
  63.8 0.2 reduce-scatter.2.cloned.1.call-start
  64.0 24.4 %select_convert_fusion = bf16[512,8192]{1,0:T(8,128)(2,1)} fusion(bf16[512,2048]{1,0:T(8,128)(2,1)S(1)} %copy-done.2, bf16[8192,2048]{1,0:T(8,128)(2,1)} %param.10, pred[8192]{0:T(1024)(128)(4,1)S(1)} %fusion.23), kind=kOutput, calls=%fused_computation | convolution fusion | flops 17188257792 | bytes 44048384 | tf_op jit(solution)/shard_map/dot_general | solution.py:70
  88.4 0.0 reduce-scatter.2.cloned.1.call-update
  88.4 0.7 copy-done.4
  89.1 0.1 select_reduce_fusion
  89.5 0.0 copy-start.3
  89.5 0.0 copy-start.8
  89.6 7.7 %fusion.14 = f32[512,2048]{1,0:T(8,128)} fusion(bf16[2048,1024]{1,0:T(8,128)(2,1)} %param.11, bf16[512,1024]{1,0:T(8,128)(2,1)S(1)} %constant_dynamic-update-slice_fusion.8, s32[1024]{0:T(1024)S(1)} %add_select_fusion.1, s32[512]{0:T(512)S(1)} %select_reduce_fusion.3), kind=kOutput, calls=%fused_computation.25 | convolution fusion | flops 2148532224 | bytes 9443328 | tf_op jit(solution)/shard_map/dot_general | solution.py:88
  97.6 4.4 fusion.13
  102.0 2.0 slice_dynamic-update-slice_fusion.6
  104.0 2.0 slice_dynamic-update-slice_fusion.5
  106.0 1.9 slice_dynamic-update-slice_fusion.4
  107.9 1.9 slice_dynamic-update-slice_fusion.3
  109.8 0.9 slice_dynamic-update-slice_fusion.2
  110.6 0.9 slice_dynamic-update-slice_fusion.1
  111.5 0.9 slice_dynamic-update-slice_fusion
  112.4 1.0 slice_dynamic-update-slice_fusion.7
  113.4 0.8 slice_dynamic-update-slice_fusion.13
  114.3 0.8 slice_dynamic-update-slice_fusion.12
  115.1 0.8 slice_dynamic-update-slice_fusion.11
  115.9 0.8 slice_dynamic-update-slice_fusion.10
  116.8 0.8 slice_dynamic-update-slice_fusion.9
  117.6 0.8 slice_dynamic-update-slice_fusion.8
  118.4 0.8 slice_dynamic-update-slice_fusion.15
  119.2 19.4 %all-gather.9.cloned.1.call-done = bf16[2048,2048]{1,0:T(8,128)(2,1)} async-done(((bf16[512,2048]{1,0:T(8,128)(2,1)}), bf16[2048,2048]{1,0:T(8,128)(2,1)}) %all-gather.9.cloned.1.call-update) | async-done | bytes 8388624 | tf_op jit(solution)/shard_map/all_gather | solution.py:77
  138.6 14.9 %multiply_bitcast_fusion.1 = f32[1,2048,1024]{1,2,0:T(8,128)} fusion(bf16[2048,2048]{1,0:T(8,128)(2,1)} %all-gather.9.cloned.1.call-done, bf16[2048,1024]{1,0:T(8,128)(2,1)} %slice_dynamic-update-slice_fusion.15, f32[1024]{0:T(1024)S(1)} %compare_select_fusion.12, s32[1024]{0:T(1024)S(1)} %add_select_fusion.1, s32[2048]{0:T(1024)S(1)} %bitcast.30), kind=kOutput, calls=%fused_computation.4 | convolution fusion | flops 8596226048 | bytes 20987904 | tf_op jit(solution)/shard_map/dot_general | solution.py:98
  153.5 9.2 %copy.15 = f32[1,2048,1024]{2,1,0:T(8,128)} copy(f32[1,2048,1024]{1,2,0:T(8,128)} %multiply_bitcast_fusion.1) | data formatting | bytes 16777216
  162.7 35.6 %all-gather.11.cloned.1.call-done = bf16[2048,2048]{1,0:T(8,128)(2,1)} async-done(((bf16[512,2048]{1,0:T(8,128)(2,1)}), bf16[2048,2048]{1,0:T(8,128)(2,1)}) %all-gather.11.cloned.1.call-update) | async-done | bytes 8388624 | tf_op jit(solution)/shard_map/all_gather | solution.py:78
  198.3 14.9 %multiply_bitcast_fusion = f32[1,1024,2048]{2,1,0:T(8,128)} fusion(bf16[2048,2048]{1,0:T(8,128)(2,1)} %all-gather.11.cloned.1.call-done, bf16[2048,1024]{1,0:T(8,128)(2,1)} %get-tuple-element.19, f32[1024]{0:T(1024)S(1)} %compare_select_fusion.12, s32[1024]{0:T(1024)S(1)} %add_select_fusion.1, s32[2048]{0:T(1024)S(1)} %bitcast.31), kind=kOutput, calls=%fused_computation.3 | convolution fusion | flops 8596226048 | bytes 20987904 | tf_op jit(solution)/shard_map/dot_general | solution.py:99
  213.2 136.2 %all-gather.5.cloned.1.call-done = bf16[512,8192]{1,0:T(8,128)(2,1)} async-done(((bf16[512,2048]{1,0:T(8,128)(2,1)}), bf16[512,8192]{1,0:T(8,128)(2,1)}) %all-gather.5.cloned.1.call-update) | async-done | bytes 8388624 | tf_op jit(solution)/shard_map/all_gather | solution.py:67
  349.4 24.9 %select_convert_fusion.1 = bf16[512,2048]{1,0:T(8,128)(2,1)} fusion(f32[512,2048]{1,0:T(8,128)} %fusion.13, bf16[512,8192]{1,0:T(8,128)(2,1)} %all-gather.5.cloned.1.call-done, bf16[8192,2048]{1,0:T(8,128)(2,1)} %param.10, pred[512]{0:T(512)(128)(4,1)S(1)} %broadcast_compare_fusion), kind=kOutput, calls=%fused_computation.19 | convolution fusion | flops 17183014912 | bytes 48235008 | tf_op jit(solution)/shard_map/dot_general | solution.py:83
  374.3 120.0 %reduce-scatter.2.cloned.1.call-done = bf16[512,2048]{1,0:T(8,128)(2,1)} async-done(((bf16[512,8192]{1,0:T(8,128)(2,1)}), bf16[512,2048]{1,0:T(8,128)(2,1)}) %reduce-scatter.2.cloned.1.call-update) | async-done | bytes 2097168 | tf_op jit(solution)/shard_map/reduce_scatter | solution.py:72
  494.3 10.3 %fusion.4 = bf16[512,2048]{1,0:T(8,128)(2,1)} fusion(f32[512,2048]{1,0:T(8,128)} %fusion.14, bf16[512,2048]{1,0:T(8,128)(2,1)} %reduce-scatter.2.cloned.1.call-done, bf16[512,2048]{1,0:T(8,128)(2,1)S(1)} %copy-done.2, bf16[8192,2048]{1,0:T(8,128)(2,1)} %param.10, s32[]{:T(128)S(6)} %select_n.128, pred[512]{0:T(512)(128)(4,1)S(1)} %broadcast_compare_fusion), kind=kOutput, calls=%fused_computation.16 | convolution fusion | flops 4300210176 | bytes 18874884 | tf_op jit(solution)/shard_map/dot_general | solution.py:74
  (32 shorter events, 0.6 us)
Async XLA Ops:
  7.2 51.1 %all-reduce.2.cloned.1.call-start = ((), (), s32[]{:S(2)}) async-start(), calls=%async_computation.2 | async-start | bytes 1048576 | tf_op jit(solution)/shard_map/psum | solution.py:63
  8.3 5.5 %copy-start.1 = (bf16[512,2048]{1,0:T(8,128)(2,1)S(1)}, bf16[512,2048]{1,0:T(8,128)(2,1)}, u32[]{:S(2)}) copy-start(bf16[512,2048]{1,0:T(8,128)(2,1)} %param.8) | copy-start | bytes 6291460
  8.3 5.5 %copy-start.7 = (bf16[2048,1024]{1,0:T(8,128)(2,1)S(1)}, bf16[2048,1024]{1,0:T(8,128)(2,1)}, u32[]{:S(2)}) copy-start(bf16[2048,1024]{1,0:T(8,128)(2,1)} %param.11) | copy-start | bytes 12582916
  13.8 3.4 copy-start.5
  13.8 3.4 copy-start.6
  17.1 84.9 %all-gather.7.cloned.1.call-start = ((), (), s32[]{:S(2)}) async-start(), calls=%async_computation.4 | async-start | bytes 1310720 | tf_op jit(solution)/shard_map/all_gather | solution.py:79
  59.3 4.7 copy-start.2
  61.8 76.8 %all-gather.9.cloned.1.call-start = ((), (), s32[]{:S(2)}) async-start(), calls=%async_computation.5 | async-start | bytes 10485760 | tf_op jit(solution)/shard_map/all_gather | solution.py:77
  62.6 135.8 %all-gather.11.cloned.1.call-start = ((), (), s32[]{:S(2)}) async-start(), calls=%async_computation.6 | async-start | bytes 10485760 | tf_op jit(solution)/shard_map/all_gather | solution.py:78
  63.2 286.3 %all-gather.5.cloned.1.call-start = ((), (), s32[]{:S(2)}) async-start(), calls=%async_computation.1 | async-start | bytes 10485760 | tf_op jit(solution)/shard_map/all_gather | solution.py:67
  63.8 430.6 %reduce-scatter.2.cloned.1.call-start = ((), (), s32[]{:S(2)}) async-start(), calls=%async_computation.3 | async-start | bytes 10485760 | tf_op jit(solution)/shard_map/reduce_scatter | solution.py:72
  88.4 0.7 copy-start.4
  89.5 7.7 %copy-start.3 = (bf16[512,1024]{1,0:T(8,128)(2,1)S(1)}, bf16[512,1024]{1,0:T(8,128)(2,1)}, u32[]{:S(2)}) copy-start(bf16[512,1024]{1,0:T(8,128)(2,1)} %get-tuple-element.17) | copy-start | bytes 3145732
  89.5 8.0 %copy-start.8 = (bf16[1024,2048]{1,0:T(8,128)(2,1)S(1)}, bf16[1024,2048]{1,0:T(8,128)(2,1)}, u32[]{:S(2)}) copy-start(bf16[1024,2048]{1,0:T(8,128)(2,1)} %param.12) | copy-start | bytes 12582916
  102.0 7.8 %copy-start = (bf16[2048,256]{1,0:T(8,128)(2,1)S(1)}, bf16[2048,256]{1,0:T(8,128)(2,1)}, u32[]{:S(2)}) copy-start(bf16[2048,256]{1,0:T(8,128)(2,1)} %all-gather.7.cloned.1.call-done) | copy-start | bytes 3145732
Sparse Core Ops, SparseCore 0:
  17.2 40.9 all-reduce.1
  62.0 16.6 all-gather.6
  80.3 58.2 all-gather.8
  140.0 58.2 all-gather.10
  199.8 149.6 all-gather.4
  351.6 142.6 reduce-scatter.1

commit v2 on v1

--- a/solution.py
+++ b/solution.py
@@ -1,6 +1,10 @@
+import functools
+
 import jax
 import jax.numpy as jnp
 from jax import lax
+from jax.experimental import pallas as pl
+from jax.experimental.pallas import tpu as pltpu
 from jax.sharding import PartitionSpec as P
 
 LARGEST_RANK = 64
@@ -11,6 +15,214 @@
 
 TRAILING = (((1,), (1,)), ((), ()))
 FIRST = (((0,), (0,)), ((), ()))
+
+
+MESH = pl.DeviceIdType.MESH
+
+
+def exchange_kernel(
+    n, chunks, cot_ref, inp_ref, w_ref, share_ref, ginp_ref, gcot_ref,
+    cot_v, wbuf, part, to_right, to_left, out_v,
+    w_sem, cot_sem, out_sem, own_sem, rs_send, rs_recv, ls_send, ls_recv, dp_send, dp_recv,
+):
+    me = lax.axis_index("tensor")
+    group = lax.axis_index("dp")
+    sibling = group + 1 - 2 * lax.rem(group, 2)
+    cross = lax.rem(group + 2, 4)
+    far = lax.rem(sibling + 2, 4)
+    right, left = jnp.minimum(me + 1, n - 1), jnp.maximum(me - 1, 0)
+    n_right, n_left = n - 1 - me, me
+    width = wbuf.shape[1]
+    rows = cot_v.shape[0]
+    feat = width * chunks
+
+    def weight_copy(i):
+        dest, _, c, _ = item(i)
+        start = pl.multiple_of(dest * feat + c * width, width)
+        return pltpu.make_async_copy(
+            w_ref.at[pl.ds(start, width), :], wbuf.at[lax.rem(i, 2)], w_sem.at[lax.rem(i, 2)]
+        )
+
+    def item(i):
+        both = jnp.minimum(n_right, n_left)
+        paired = 2 * both * chunks
+        in_pair = i < paired
+        rest = jnp.maximum(i - paired, 0)
+        p = jnp.where(in_pair, i // (2 * chunks), both + rest // chunks)
+        c = jnp.where(in_pair, lax.rem(i, 2 * chunks) // 2, lax.rem(rest, chunks))
+        is_right = jnp.where(in_pair, lax.rem(i, 2), jnp.where(n_right > n_left, 0, 1))
+        own = i >= (n - 1) * chunks
+        kind = jnp.where(own, 2, is_right)
+        dest = jnp.where(own, me, jnp.where(is_right == 0, n - 1 - p, p))
+        return dest, p, c, kind
+
+    pltpu.make_async_copy(cot_ref, cot_v, cot_sem).start()
+    weight_copy(0).start()
+
+    barrier = pltpu.get_barrier_semaphore()
+    for peer in (sibling, cross):
+        pl.semaphore_signal(barrier, inc=1, device_id={"dp": peer}, device_id_type=MESH)
+
+    @pl.when(me > 0)
+    def _():
+        pl.semaphore_signal(barrier, inc=1, device_id={"tensor": left}, device_id_type=MESH)
+
+    @pl.when(me < n - 1)
+    def _():
+        pl.semaphore_signal(barrier, inc=1, device_id={"tensor": right}, device_id_type=MESH)
+
+    edges = jnp.where(me > 0, 1, 0) + jnp.where(me < n - 1, 1, 0)
+    pl.semaphore_wait(barrier, 2 + edges)
+
+    def dp_copy(k, src, dst, slot, peer):
+        return pltpu.make_async_remote_copy(
+            src_ref=src, dst_ref=dst.at[slot], send_sem=dp_send.at[k], recv_sem=dp_recv.at[k],
+            device_id={"dp": peer}, device_id_type=MESH,
+        )
+
+    def right_copy(p, c):
+        return pltpu.make_async_remote_copy(
+            src_ref=to_right.at[p, c], dst_ref=to_right.at[p, c],
+            send_sem=rs_send.at[p, c], recv_sem=rs_recv.at[p, c],
+            device_id={"tensor": right}, device_id_type=MESH,
+        )
+
+    def left_copy(p, c):
+        return pltpu.make_async_remote_copy(
+            src_ref=to_left.at[p, c], dst_ref=to_left.at[p, c],
+            send_sem=ls_send.at[p, c], recv_sem=ls_recv.at[p, c],
+            device_id={"tensor": left}, device_id_type=MESH,
+        )
+
+    for k, (src, dst) in enumerate(((inp_ref, ginp_ref), (cot_ref, gcot_ref))):
+        pltpu.make_async_copy(src, dst.at[group], own_sem.at[k]).start()
+        dp_copy(3 * k, src, dst, group, cross).start()
+        dp_copy(3 * k + 1, src, dst, group, sibling).start()
+
+    pltpu.make_async_copy(cot_ref, cot_v, cot_sem).wait()
+
+    def step(i, carry):
+        dest, p, c, kind = item(i)
+        weight_copy(i).wait()
+
+        @pl.when(i + 1 < n * chunks)
+        def _():
+            weight_copy(i + 1).start()
+
+        part[...] = lax.dot_general(
+            cot_v[...], wbuf[lax.rem(i, 2)], TRAILING, preferred_element_type=jnp.float32
+        )
+
+        @pl.when(kind == 0)
+        def _():
+            @pl.when(me > 0)
+            def _():
+                right_copy(p, c).wait_recv()
+                part[...] += to_right[p, c].astype(jnp.float32)
+
+            to_right[p, c] = part[...].astype(jnp.bfloat16)
+            right_copy(p, c).start()
+
+        @pl.when(kind == 1)
+        def _():
+            @pl.when(me < n - 1)
+            def _():
+                left_copy(p, c).wait_recv()
+                part[...] += to_left[p, c].astype(jnp.float32)
+
+            to_left[p, c] = part[...].astype(jnp.bfloat16)
+            left_copy(p, c).start()
+
+        @pl.when(kind == 2)
+        def _():
+            @pl.when(me > 0)
+            def _():
+                right_copy(n_right, c).wait_recv()
+                part[...] += to_right[n_right, c].astype(jnp.float32)
+
+            @pl.when(me < n - 1)
+            def _():
+                left_copy(n_left, c).wait_recv()
+                part[...] += to_left[n_left, c].astype(jnp.float32)
+
+            out_v[c] = part[...]
+            start = pl.multiple_of(c * width, width)
+            pltpu.make_async_copy(
+                out_v.at[c], share_ref.at[:, pl.ds(start, width)], out_sem.at[c]
+            ).start()
+
+        return carry
+
+    lax.fori_loop(0, (n - 1) * chunks, step, 0)
+
+    for k, (src, dst) in enumerate(((inp_ref, ginp_ref), (cot_ref, gcot_ref))):
+        dp_copy(3 * k, src, dst, cross, cross).wait_recv()
+        dp_copy(3 * k + 2, dst.at[cross], dst, cross, sibling).start()
+
+    lax.fori_loop((n - 1) * chunks, n * chunks, step, 0)
+
+    def drain_right(j, carry):
+        right_copy(j // chunks, lax.rem(j, chunks)).wait_send()
+        return carry
+
+    def drain_left(j, carry):
+        left_copy(j // chunks, lax.rem(j, chunks)).wait_send()
+        return carry
+
+    lax.fori_loop(0, n_right * chunks, drain_right, 0)
+    lax.fori_loop(0, n_left * chunks, drain_left, 0)
+    for k, (src, dst) in enumerate(((inp_ref, ginp_ref), (cot_ref, gcot_ref))):
+        dp_copy(3 * k, src, dst, group, cross).wait_send()
+        dp_copy(3 * k + 1, src, dst, group, sibling).wait_send()
+        dp_copy(3 * k + 1, src, dst, sibling, sibling).wait_recv()
+        dp_copy(3 * k + 2, dst.at[cross], dst, cross, sibling).wait_send()
+        dp_copy(3 * k + 2, dst.at[cross], dst, far, sibling).wait_recv()
+        pltpu.make_async_copy(src, dst.at[group], own_sem.at[k]).wait()
+    for c in range(chunks):
+        pltpu.make_async_copy(
+            out_v.at[c], share_ref.at[:, pl.ds(c * width, width)], out_sem.at[c]
+        ).wait()
+
+
+def exchange(n, inputs, cotangent, weight):
+    rows, feat = inputs.shape
+    width = min(512, feat)
+    chunks = feat // width
+    slots = n - 1
+    ring = pltpu.VMEM((slots, chunks, rows, width), jnp.bfloat16)
+    sems = pltpu.SemaphoreType.DMA((slots, chunks))
+    return pl.pallas_call(
+        functools.partial(exchange_kernel, n, chunks),
+        out_shape=(
+            jax.ShapeDtypeStruct((rows, feat), jnp.float32),
+            jax.ShapeDtypeStruct((4, rows, feat), jnp.bfloat16),
+            jax.ShapeDtypeStruct((4, rows, feat), jnp.bfloat16),
+        ),
+        in_specs=[pl.BlockSpec(memory_space=pl.ANY)] * 3,
+        out_specs=(pl.BlockSpec(memory_space=pl.ANY),) * 3,
+        scratch_shapes=[
+            pltpu.VMEM((rows, cotangent.shape[1]), jnp.bfloat16),
+            pltpu.VMEM((2, width, weight.shape[1]), jnp.bfloat16),
+            pltpu.VMEM((rows, width), jnp.float32),
+            ring,
+            ring,
+            pltpu.VMEM((chunks, rows, width), jnp.float32),
+            pltpu.SemaphoreType.DMA((2,)),
+            pltpu.SemaphoreType.DMA,
+            pltpu.SemaphoreType.DMA((chunks,)),
+            pltpu.SemaphoreType.DMA((2,)),
+            sems, sems, sems, sems,
+            pltpu.SemaphoreType.DMA((6,)),
+            pltpu.SemaphoreType.DMA((6,)),
+        ],
+        compiler_params=pltpu.CompilerParams(
+            collective_id=0, has_side_effects=True, vmem_limit_bytes=40 * 1024 * 1024
+        ),
+        cost_estimate=pl.CostEstimate(
+            flops=2 * rows * cotangent.shape[1] * weight.shape[0],
+            bytes_accessed=400 * 1024 * 1024, transcendentals=0,
+        ),
+    )(cotangent, inputs, weight)
 
 
 def fold_columns(values, match):
@@ -65,17 +277,11 @@
     scaled_back_f = (coef_folded * folded[:, LANES:]).astype(jnp.bfloat16)
 
     all_inputs = lax.all_gather(inputs, "tensor", axis=1, tiled=True)
-    mine = lax.axis_index("tensor")
-    block = jnp.arange(weight.shape[0], dtype=jnp.int32) // feature_local
-    frozen_back = lax.dot_general(cotangent, weight, TRAILING, preferred_element_type=jnp.float32)
-    others = jnp.where((block == mine)[None, :], 0.0, frozen_back).astype(jnp.bfloat16)
-    others_share = lax.psum_scatter(others, "tensor", scatter_dimension=1, tiled=True)
-    own_weight = lax.dynamic_slice_in_dim(weight, mine * feature_local, feature_local, 0)
-    own_share = lax.dot_general(cotangent, own_weight, TRAILING, preferred_element_type=jnp.float32)
-    frozen_share = own_share + others_share.astype(jnp.float32)
-
-    group_inputs = lax.all_gather(inputs, "dp", axis=0, tiled=True)
-    group_cotangent = lax.all_gather(cotangent, "dp", axis=0, tiled=True)
+    frozen_share, group_inputs, group_cotangent = exchange(
+        lax.axis_size("tensor"), inputs, cotangent, weight
+    )
+    group_inputs = group_inputs.reshape(-1, feature_local)
+    group_cotangent = group_cotangent.reshape(-1, cotangent.shape[1])
     both = lax.all_gather(
         jnp.concatenate([scaled_down_f, scaled_back_f], axis=1), "dp", axis=0, tiled=True
     )

time: 512 us -> 388 us (0.76)
  waiting for transfers between devices: 354 us -> 40 us
  Pallas kernels: 0 us -> 245 us
  matrix products: 109 us -> 64.8 us
  local copies, waits for them, and re-layouts: 27.7 us -> 9.92 us
    pallas_call x0 -> x1, Pallas kernels: none -> 245 us  [exchange(): pl.pallas_call(functools.partial(exchange_kernel, n, chunks), out_shape=(...]
    all_gather x1, waiting for transfers between devices: 136 us -> 0.01 us  [local(): all_inputs = lax.all_gather(inputs, 'tensor', axis=1, tiled=True)]
    reduce_scatter x1 -> x0, waiting for transfers between devices: 120 us -> none  [local(): lax.psum_scatter(others, 'tensor', scatter_dimension=1, tiled=True)]
    all_gather x2 -> x0, waiting for transfers between devices: 55 us -> none  [the longest x1 35.6 us: local(): group_cotangent = lax.all_gather(cotangent, 'dp', axis=0, tiled=True)]
    dot_general x2 -> x0, matrix products: 34.6 us -> none  [the longest x1 24.4 us: local(): lax.dot_general(cotangent, weight, TRAILING, preferred_element_type=jnp.f...]
    unnamed x45 -> x56, local copies, waits for them, and re-layouts: 25.8 us -> 9.36 us
  transfers between devices with their start and end apart: 6 -> 3, of which waited for: 5 -> 1; matrix products, arithmetic and copies ran while one was open for 23% -> 11% of each run, Pallas kernels for 0% -> 64%
where the time goes in v2:
time: 388 us; the launch traced here: 382 us
  Pallas kernels  245 us (63%)
  matrix products  64.8 us (17%)
  waiting for transfers between devices  40 us (10%)
  between operations  14.2 us (4%)
  local copies, waits for them, and re-layouts  9.92 us (3%)
  other arithmetic  8.01 us (2%)
    pallas_call x1, Pallas kernels, exchange(): pl.pallas_call(functools.partial(exchange_kernel, n, chunks), out_shape=(...  245 us
    psum x1, waiting for transfers between devices, local(): folded = lax.psum(folded, 'tensor')  39.3 us
    dot_general x1, matrix products, local(): jnp.dot(all_inputs, weight, preferred_element_type=jnp.float32)  24.9 us
    dot_general x1, matrix products, local(): lax.dot_general(down_all, group_cotangent, FIRST, preferred_element_type=...  12.1 us
    dot_general x1, matrix products, local(): lax.dot_general(group_inputs, back_all, FIRST, preferred_element_type=jnp...  11.9 us
    unnamed x56, local copies, waits for them, and re-layouts  9.36 us
  transfers between devices with their start and end apart: 3, of which 1 were waited for; matrix products, arithmetic and copies ran while one was open for 11% of the time, Pallas kernels for 64%

profile of v2, /device:TPU:0, one launch (start us, length us, event | category | flops | bytes accessed | tf_op | source)
XLA Modules:
  0.0 382.4 jit_solution(6555908566789710808)
XLA Ops:
  7.2 0.0 all-reduce.2.cloned.1.call-start
  7.2 0.9 reduce_window_sum.11
  8.1 0.1 convert_reduce_fusion
  8.2 0.1 select_reduce_fusion.3
  8.3 5.3 %compare_select_fusion.4 = f32[512,1024]{1,0:T(8,128)S(1)} fusion(bf16[512,2048]{1,0:T(8,128)(2,1)} %cot_ref.1, bf16[1024,2048]{1,0:T(8,128)(2,1)} %param.12, s32[1024]{0:T(1024)S(1)} %add_select_fusion, s32[512]{0:T(512)S(1)} %select_reduce_fusion.3), kind=kOutput, calls=%fused_computation.6 | convolution fusion | flops 2148532224 | bytes 8394752 | tf_op jit(solution)/shard_map/dot_general | solution.py:271
  13.6 0.1 slice_add_fusion
  13.8 0.0 copy-done
  13.8 0.0 copy-done.9
  13.8 0.0 copy-start.6
  13.8 0.0 copy-start.7
  13.8 2.3 compare_select_fusion.5
  16.1 0.1 slice_add_fusion.7
  16.2 0.8 pad_maximum_fusion
  17.1 0.0 all-reduce.2.cloned.1.call-update
  17.1 0.0 all-gather.5.cloned.1.call-start
  17.1 0.0 copy-done.6
  17.2 0.0 copy-done.7
  17.2 0.1 select_reduce_fusion.1
  17.3 0.0 copy-start.5
  17.3 0.0 copy-start.1
  17.3 1.6 compare_select_fusion.6
  18.9 39.3 %all-reduce.2.cloned.1.call-done = f32[512,256]{1,0:T(8,128)} async-done(((f32[512,256]{1,0:T(8,128)}), f32[512,256]{1,0:T(8,128)}) %all-reduce.2.cloned.1.call-update) | async-done | bytes 524304 | tf_op jit(solution)/shard_map/psum | solution.py:275
  58.2 1.7 constant_dynamic-update-slice_fusion.15
  60.0 1.6 constant_dynamic-update-slice_fusion.7
  61.6 0.7 pad_maximum_fusion.1
  62.3 0.0 all-gather.5.cloned.1.call-update
  62.4 0.0 all-gather.3.cloned.1.call-start
  62.4 0.7 all-gather.3.cloned.1.call-update
  63.1 0.0 copy-done.5
  63.1 0.1 select_reduce_fusion
  63.2 0.0 copy-done.1
  63.3 0.0 copy-start.2
  63.3 1.6 copy-done.2
  64.9 245.3 %shard_map.111 = (f32[512,2048]{1,0:T(8,128)S(1)}, bf16[4,512,2048]{2,1,0:T(8,128)(2,1)}, bf16[4,512,2048]{2,1,0:T(8,128)(2,1)}) custom-call(bf16[512,2048]{1,0:T(8,128)(2,1)S(1)} %copy-done.2, bf16[512,2048]{1,0:T(8,128)(2,1)S(1)} %copy-done.1, bf16[8192,2048]{1,0:T(8,128)(2,1)} %w_ref.1), custom_call_target="tpu_custom_call" | custom-call | flops 17179869184 | bytes 419430400 | tf_op jit(solution)/shard_map/pallas_call | solution.py:194
  310.5 0.0 copy-done.4
  310.8 0.0 copy-done.8
  310.9 0.0 copy-start.10
  310.9 4.4 %fusion.6 = f32[512,2048]{1,0:T(8,128)} fusion(bf16[1024,2048]{1,0:T(8,128)(2,1)S(1)} %copy-done.8, bf16[512,1024]{1,0:T(8,128)(2,1)S(1)} %constant_dynamic-update-slice_fusion, s32[1024]{0:T(1024)S(1)} %add_select_fusion, s32[512]{0:T(512)S(1)} %select_reduce_fusion.3), kind=kOutput, calls=%fused_computation.18 | convolution fusion | flops 2148532224 | bytes 9443328 | tf_op jit(solution)/shard_map/dot_general | solution.py:292
  315.3 0.0 copy-done.10
  315.3 3.8 select_convert_fusion
  319.1 1.3 slice_dynamic-update-slice_fusion.6
  320.3 0.0 slice-start.2
  320.3 1.4 slice_dynamic-update-slice_fusion.5
  321.7 1.2 slice_dynamic-update-slice_fusion.4
  323.0 1.2 slice_dynamic-update-slice_fusion.3
  324.2 0.2 slice_dynamic-update-slice_fusion.2
  324.4 0.2 slice_dynamic-update-slice_fusion.1
  324.6 0.2 slice_dynamic-update-slice_fusion
  324.8 0.0 slice-start.3
  324.8 0.3 slice_dynamic-update-slice_fusion.7
  325.1 0.2 slice_dynamic-update-slice_fusion.13
  325.3 0.2 slice_dynamic-update-slice_fusion.12
  325.5 0.2 slice_dynamic-update-slice_fusion.11
  325.6 0.2 slice_dynamic-update-slice_fusion.10
  325.8 0.2 slice_dynamic-update-slice_fusion.9
  326.0 0.0 slice-start
  326.0 0.2 slice_dynamic-update-slice_fusion.8
  326.2 0.2 slice_dynamic-update-slice_fusion.15
  326.4 0.0 slice-done.2
  326.4 0.5 slice-done.3
  326.9 11.9 %multiply_bitcast_fusion.1 = f32[1,2048,1024]{2,1,0:T(8,128)} fusion(bf16[2048,2048]{1,0:T(8,128)(2,1)S(1)} %bitcast.26, bf16[2048,1024]{1,0:T(8,128)(2,1)S(1)} %slice_dynamic-update-slice_fusion.15, f32[1024]{0:T(1024)S(1)} %compare_select_fusion.12, s32[1024]{0:T(1024)S(1)} %add_select_fusion, s32[2048]{0:T(1024)S(1)} %bitcast.19), kind=kOutput, calls=%fused_computation.3 | convolution fusion | flops 8596226048 | bytes 20987904 | tf_op jit(solution)/shard_map/dot_general | solution.py:304
  338.9 0.0 slice-done
  338.9 12.1 %multiply_bitcast_fusion = f32[1,1024,2048]{2,1,0:T(8,128)} fusion(bf16[2048,2048]{1,0:T(8,128)(2,1)S(1)} %bitcast.23, bf16[2048,1024]{1,0:T(8,128)(2,1)S(1)} %get-tuple-element.17, f32[1024]{0:T(1024)S(1)} %compare_select_fusion.12, s32[1024]{0:T(1024)S(1)} %add_select_fusion, s32[2048]{0:T(1024)S(1)} %bitcast.20), kind=kOutput, calls=%fused_computation.2 | convolution fusion | flops 8596226048 | bytes 20987904 | tf_op jit(solution)/shard_map/dot_general | solution.py:305
  351.0 24.9 %select_convert_fusion.1 = bf16[512,2048]{1,0:T(8,128)(2,1)} fusion(f32[512,2048]{1,0:T(8,128)} %fusion.6, bf16[512,8192]{1,0:T(8,128)(2,1)} %all-gather.3.cloned.1.call-done, bf16[8192,2048]{1,0:T(8,128)(2,1)} %w_ref.1, pred[512]{0:T(512)(128)(4,1)S(1)} %broadcast_compare_fusion), kind=kOutput, calls=%fused_computation.13 | convolution fusion | flops 17183014912 | bytes 48235008 | tf_op jit(solution)/shard_map/dot_general | solution.py:289
  (34 shorter events, 0.6 us)
Async XLA Ops:
  7.2 51.1 %all-reduce.2.cloned.1.call-start = ((), (), s32[]{:S(2)}) async-start(), calls=%async_computation.1 | async-start | bytes 1048576 | tf_op jit(solution)/shard_map/psum | solution.py:275
  8.3 5.5 %copy-start = (bf16[512,2048]{1,0:T(8,128)(2,1)S(1)}, bf16[512,2048]{1,0:T(8,128)(2,1)}, u32[]{:S(2)}) copy-start(bf16[512,2048]{1,0:T(8,128)(2,1)} %inp_ref.1) | copy-start | bytes 6291460
  8.3 5.5 %copy-start.9 = (bf16[2048,1024]{1,0:T(8,128)(2,1)S(1)}, bf16[2048,1024]{1,0:T(8,128)(2,1)}, u32[]{:S(2)}) copy-start(bf16[2048,1024]{1,0:T(8,128)(2,1)} %param.11) | copy-start | bytes 12582916
  13.8 3.4 copy-start.6
  13.8 3.4 copy-start.7
  17.1 302.0 %all-gather.5.cloned.1.call-start = ((), (), s32[]{:S(2)}) async-start(), calls=%async_computation.2 | async-start | bytes 1310720 | tf_op jit(solution)/shard_map/all_gather | solution.py:285
  17.3 45.8 %copy-start.5 = (s32[4,16]{1,0:T(4,128)S(1)}, s32[4,16]{1,0:T(4,128)}, u32[]{:S(2)}) copy-start(s32[4,16]{1,0:T(4,128)} %param.13) | copy-start | bytes 772
  17.3 46.0 %copy-start.1 = (bf16[512,2048]{1,0:T(8,128)(2,1)S(1)}, bf16[512,2048]{1,0:T(8,128)(2,1)}, u32[]{:S(2)}) copy-start(bf16[512,2048]{1,0:T(8,128)(2,1)} %inp_ref.1) | copy-start | bytes 6291460
  62.4 288.6 %all-gather.3.cloned.1.call-start = ((), (), s32[]{:S(2)}) async-start(), calls=%async_computation | async-start | bytes 10485760 | tf_op jit(solution)/shard_map/all_gather | solution.py:279
  63.3 1.6 copy-start.2
  64.9 245.7 %copy-start.4 = (bf16[512,1024]{1,0:T(8,128)(2,1)S(1)}, bf16[512,1024]{1,0:T(8,128)(2,1)}, u32[]{:S(2)}) copy-start(bf16[512,1024]{1,0:T(8,128)(2,1)} %get-tuple-element.15) | copy-start | bytes 3145732
  64.9 246.0 %copy-start.8 = (bf16[1024,2048]{1,0:T(8,128)(2,1)S(1)}, bf16[1024,2048]{1,0:T(8,128)(2,1)}, u32[]{:S(2)}) copy-start(bf16[1024,2048]{1,0:T(8,128)(2,1)} %param.12) | copy-start | bytes 12582916
  310.9 4.4 %copy-start.10 = (bf16[2048,1024]{1,0:T(8,128)(2,1)S(1)}, bf16[2048,1024]{1,0:T(8,128)(2,1)}, u32[]{:S(2)}) copy-start(bf16[2048,1024]{1,0:T(8,128)(2,1)} %param.11) | copy-start | bytes 12582916
  319.0 5.1 %copy-start.3 = (bf16[2048,256]{1,0:T(8,128)(2,1)S(1)}, bf16[2048,256]{1,0:T(8,128)(2,1)}, u32[]{:S(2)}) copy-start(bf16[2048,256]{1,0:T(8,128)(2,1)} %all-gather.5.cloned.1.call-done) | copy-start | bytes 3145732
  320.3 6.1 %slice-start.2 = ((s8[8388608]{0:T(1024)(128)(4,1)}), s8[4194304]{0:T(1024)(128)(4,1)S(1)}, s32[]{:S(2)}) async-start(s8[8388608]{0:T(1024)(128)(4,1)} %bitcast.24), calls=%async_computation.5 | async-start | bytes 8388608
  324.8 2.2 slice-start.3
  326.0 12.8 %slice-start = ((s8[8388608]{0:T(1024)(128)(4,1)}), s8[4194304]{0:T(1024)(128)(4,1)S(1)}, s32[]{:S(2)}) async-start(s8[8388608]{0:T(1024)(128)(4,1)} %bitcast.21), calls=%async_computation.3 | async-start | bytes 8388608
  326.9 11.9 %slice-start.1 = ((s8[8388608]{0:T(1024)(128)(4,1)}), s8[4194304]{0:T(1024)(128)(4,1)S(1)}, s32[]{:S(2)}) async-start(s8[8388608]{0:T(1024)(128)(4,1)} %bitcast.21), calls=%async_computation.4 | async-start | bytes 8388608
Sparse Core Ops, SparseCore 0:
  17.2 40.9 all-reduce.1
  62.5 22.4 all-gather.4
  86.6 250.4 all-gather.2

commit v3 on v2

--- a/solution.py
+++ b/solution.py
@@ -21,9 +21,10 @@
 
 
 def exchange_kernel(
-    n, chunks, cot_ref, inp_ref, w_ref, share_ref, ginp_ref, gcot_ref,
-    cot_v, wbuf, part, to_right, to_left, out_v,
+    n, chunks, cot_ref, inp_ref, w_ref, share_ref, front_ref, ginp_ref, gcot_ref,
+    cot_v, wbuf, part, to_right, to_left, out_v, x_v, fbuf, acc,
     w_sem, cot_sem, out_sem, own_sem, rs_send, rs_recv, ls_send, ls_recv, dp_send, dp_recv,
+    x_sem, f_sem, acc_sem, xr_send, xr_recv, xl_send, xl_recv,
 ):
     me = lax.axis_index("tensor")
     group = lax.axis_index("dp")
@@ -56,6 +57,7 @@
         dest = jnp.where(own, me, jnp.where(is_right == 0, n - 1 - p, p))
         return dest, p, c, kind
 
+    pltpu.make_async_copy(inp_ref, x_v.at[me], x_sem).start()
     pltpu.make_async_copy(cot_ref, cot_v, cot_sem).start()
     weight_copy(0).start()
 
@@ -94,6 +96,64 @@
             device_id={"tensor": left}, device_id_type=MESH,
         )
 
+    def pass_right(r):
+        block = jnp.maximum(me - r, 0)
+        return pltpu.make_async_remote_copy(
+            src_ref=x_v.at[block], dst_ref=x_v.at[block],
+            send_sem=xr_send.at[r], recv_sem=xr_recv.at[r],
+            device_id={"tensor": right}, device_id_type=MESH,
+        )
+
+    def pass_left(r):
+        block = jnp.minimum(me + r, n - 1)
+        return pltpu.make_async_remote_copy(
+            src_ref=x_v.at[block], dst_ref=x_v.at[block],
+            send_sem=xl_send.at[r], recv_sem=xl_recv.at[r],
+            device_id={"tensor": left}, device_id_type=MESH,
+        )
+
+    def front_copy(block, c):
+        start = pl.multiple_of(block * feat + c * width, width)
+        return pltpu.make_async_copy(
+            w_ref.at[pl.ds(start, width), :], fbuf.at[lax.rem(c, 2)], f_sem.at[lax.rem(c, 2)]
+        )
+
+    def front(block):
+        front_copy(block, 0).start()
+
+        def chunk(c, carry):
+            front_copy(block, c).wait()
+
+            @pl.when(c + 1 < chunks)
+            def _():
+                front_copy(block, c + 1).start()
+
+            columns = pl.ds(pl.multiple_of(c * width, width), width)
+
+            def rows_of(h, inner):
+                at = pl.ds(pl.multiple_of(h * tall, tall), tall)
+                acc[at, :] += jnp.dot(
+                    x_v[block, at, columns], fbuf[lax.rem(c, 2)],
+                    preferred_element_type=jnp.float32,
+                )
+                return inner
+
+            lax.fori_loop(0, rows // tall, rows_of, 0)
+            return carry
+
+        lax.fori_loop(0, chunks, chunk, 0)
+
+    tall = rows // 2
+    pltpu.make_async_copy(inp_ref, x_v.at[me], x_sem).wait()
+
+    @pl.when(me < n - 1)
+    def _():
+        pass_right(0).start()
+
+    @pl.when(me > 0)
+    def _():
+        pass_left(0).start()
+
     for k, (src, dst) in enumerate(((inp_ref, ginp_ref), (cot_ref, gcot_ref))):
         pltpu.make_async_copy(src, dst.at[group], own_sem.at[k]).start()
         dp_copy(3 * k, src, dst, group, cross).start()
@@ -153,7 +213,45 @@
 
         return carry
 
-    lax.fori_loop(0, (n - 1) * chunks, step, 0)
+    acc[...] = jnp.zeros_like(acc)
+    lax.fori_loop(0, chunks, step, 0)
+    front(me)
+
+    def turn(r, carry):
+        from_left, from_right = r <= me, r <= n_right
+
+        @pl.when(from_left)
+        def _():
+            pass_right(r - 1).wait_recv()
+
+            @pl.when(me < n - 1)
+            def _():
+                pass_right(r).start()
+
+        @pl.when(from_right)
+        def _():
+            pass_left(r - 1).wait_recv()
+
+            @pl.when(me > 0)
+            def _():
+                pass_left(r).start()
+
+        @pl.when(r < n - 1)
+        def _():
+            lax.fori_loop(r * chunks, (r + 1) * chunks, step, 0)
+
+        @pl.when(from_left)
+        def _():
+            front(jnp.maximum(me - r, 0))
+
+        @pl.when(from_right)
+        def _():
+            front(jnp.minimum(me + r, n - 1))
+
+        return carry
+
+    lax.fori_loop(1, n, turn, 0)
+    pltpu.make_async_copy(acc, front_ref, acc_sem).start()
 
     for k, (src, dst) in enumerate(((inp_ref, ginp_ref), (cot_ref, gcot_ref))):
         dp_copy(3 * k, src, dst, cross, cross).wait_recv()
@@ -169,6 +267,23 @@
         left_copy(j // chunks, lax.rem(j, chunks)).wait_send()
         return carry
 
+    def drain_pass_right(r, carry):
+        pass_right(r).wait_send()
+        return carry
+
+    def drain_pass_left(r, carry):
+        pass_left(r).wait_send()
+        return carry
+
+    @pl.when(me < n - 1)
+    def _():
+        lax.fori_loop(0, me + 1, drain_pass_right, 0)
+
+    @pl.when(me > 0)
+    def _():
+        lax.fori_loop(0, n_right + 1, drain_pass_left, 0)
+
+    pltpu.make_async_copy(acc, front_ref, acc_sem).wait()
     lax.fori_loop(0, n_right * chunks, drain_right, 0)
     lax.fori_loop(0, n_left * chunks, drain_left, 0)
     for k, (src, dst) in enumerate(((inp_ref, ginp_ref), (cot_ref, gcot_ref))):
@@ -195,11 +310,12 @@
         functools.partial(exchange_kernel, n, chunks),
         out_shape=(
             jax.ShapeDtypeStruct((rows, feat), jnp.float32),
+            jax.ShapeDtypeStruct((rows, weight.shape[1]), jnp.float32),
             jax.ShapeDtypeStruct((4, rows, feat), jnp.bfloat16),
             jax.ShapeDtypeStruct((4, rows, feat), jnp.bfloat16),
         ),
         in_specs=[pl.BlockSpec(memory_space=pl.ANY)] * 3,
-        out_specs=(pl.BlockSpec(memory_space=pl.ANY),) * 3,
+        out_specs=(pl.BlockSpec(memory_space=pl.ANY),) * 4,
         scratch_shapes=[
             pltpu.VMEM((rows, cotangent.shape[1]), jnp.bfloat16),
             pltpu.VMEM((2, width, weight.shape[1]), jnp.bfloat16),
@@ -207,6 +323,9 @@
             ring,
             ring,
             pltpu.VMEM((chunks, rows, width), jnp.float32),
+            pltpu.VMEM((n, rows, feat), jnp.bfloat16),
+            pltpu.VMEM((2, width, weight.shape[1]), jnp.bfloat16),
+            pltpu.VMEM((rows, weight.shape[1]), jnp.float32),
             pltpu.SemaphoreType.DMA((2,)),
             pltpu.SemaphoreType.DMA,
             pltpu.SemaphoreType.DMA((chunks,)),
@@ -214,12 +333,19 @@
             sems, sems, sems, sems,
             pltpu.SemaphoreType.DMA((6,)),
             pltpu.SemaphoreType.DMA((6,)),
+            pltpu.SemaphoreType.DMA,
+            pltpu.SemaphoreType.DMA((2,)),
+            pltpu.SemaphoreType.DMA,
+            pltpu.SemaphoreType.DMA((slots,)),
+            pltpu.SemaphoreType.DMA((slots,)),
+            pltpu.SemaphoreType.DMA((slots,)),
+            pltpu.SemaphoreType.DMA((slots,)),
         ],
         compiler_params=pltpu.CompilerParams(
-            collective_id=0, has_side_effects=True, vmem_limit_bytes=40 * 1024 * 1024
+            collective_id=0, has_side_effects=True, vmem_limit_bytes=50 * 1024 * 1024
         ),
         cost_estimate=pl.CostEstimate(
-            flops=2 * rows * cotangent.shape[1] * weight.shape[0],
+            flops=4 * rows * cotangent.shape[1] * weight.shape[0],
             bytes_accessed=400 * 1024 * 1024, transcendentals=0,
         ),
     )(cotangent, inputs, weight)
@@ -276,8 +402,7 @@
     scaled_down_f = (coef_folded * folded[:, :LANES]).astype(jnp.bfloat16)
     scaled_back_f = (coef_folded * folded[:, LANES:]).astype(jnp.bfloat16)
 
-    all_inputs = lax.all_gather(inputs, "tensor", axis=1, tiled=True)
-    frozen_share, group_inputs, group_cotangent = exchange(
+    frozen_share, frozen_output, group_inputs, group_cotangent = exchange(
         lax.axis_size("tensor"), inputs, cotangent, weight
     )
     group_inputs = group_inputs.reshape(-1, feature_local)
@@ -286,7 +411,6 @@
         jnp.concatenate([scaled_down_f, scaled_back_f], axis=1), "dp", axis=0, tiled=True
     )
 
-    frozen_output = jnp.dot(all_inputs, weight, preferred_element_type=jnp.float32)
     scaled_down = spread_columns(scaled_down_f, match)
     scaled_back = spread_columns(scaled_back_f, match)
     merged = frozen_output + jnp.dot(scaled_down, up_weight_maps, preferred_element_type=jnp.float32)

time: 388 us -> 365 us (0.941); the launches traced: 382 us -> 363 us
  Pallas kernels: 245 us -> 286 us
  waiting for transfers between devices: 40 us -> 5.68 us
  matrix products: 64.8 us -> 42.8 us
    pallas_call x1, Pallas kernels: 245 us -> 286 us  [exchange(): pl.pallas_call(functools.partial(exchange_kernel, n, chunks), out_shape=(...]
    psum x1, waiting for transfers between devices: 39.3 us -> 0.02 us  [local(): folded = lax.psum(folded, 'tensor')]
    dot_general x1 -> x0, matrix products: 24.9 us -> none  [local(): jnp.dot(all_inputs, weight, preferred_element_type=jnp.float32)]
    all_gather x1, waiting for transfers between devices: 0.01 us -> 5.62 us  [local(): lax.all_gather(jnp.concatenate([scaled_down_f, scaled_back_f], axis=1), '...]
    unnamed x56 -> x52, local copies, waits for them, and re-layouts: 9.36 us -> 8.24 us
  transfers between devices with their start and end apart: 3 -> 2, of which waited for: 1 -> 1; matrix products, arithmetic and copies ran while one was open for 11% -> 3% of each run, Pallas kernels for 64% -> 79%
where the time goes in v3:
time: 365 us; the launch traced here: 363 us
  Pallas kernels  286 us (78%)
  matrix products  42.8 us (12%)
  between operations  14.5 us (4%)
  local copies, waits for them, and re-layouts  8.81 us (2%)
  waiting for transfers between devices  5.68 us (2%)
  other arithmetic  5.52 us (2%)
    pallas_call x1, Pallas kernels, exchange(): pl.pallas_call(functools.partial(exchange_kernel, n, chunks), out_shape=(...  286 us
    dot_general x1, matrix products, local(): lax.dot_general(down_all, group_cotangent, FIRST, preferred_element_type=...  12.1 us
    dot_general x1, matrix products, local(): lax.dot_general(group_inputs, back_all, FIRST, preferred_element_type=jnp...  11.9 us
    unnamed x52, local copies, waits for them, and re-layouts  8.24 us
    dot_general x1, matrix products, local(): jnp.dot(scaled_down, up_weight_maps, preferred_element_type=jnp.float32)  7.31 us
  transfers between devices with their start and end apart: 2, of which 1 were waited for; matrix products, arithmetic and copies ran while one was open for 3% of the time, Pallas kernels for 79%

profile of v3, /device:TPU:0, one launch (start us, length us, event | category | flops | bytes accessed | tf_op | source)
XLA Modules:
  0.0 363.4 jit_solution(11417015309079289728)
XLA Ops:
  7.2 0.0 all-reduce.2.cloned.1.call-start
  7.2 0.9 reduce_window_sum.11
  8.1 0.1 convert_reduce_fusion
  8.2 0.1 select_reduce_fusion.3
  8.3 0.0 copy-start.5
  8.3 0.0 copy-start.7
  8.3 5.3 %compare_select_fusion.4 = f32[512,1024]{1,0:T(8,128)S(1)} fusion(bf16[512,2048]{1,0:T(8,128)(2,1)} %cot_ref.1, bf16[1024,2048]{1,0:T(8,128)(2,1)} %param.12, s32[1024]{0:T(1024)S(1)} %add_select_fusion, s32[512]{0:T(512)S(1)} %select_reduce_fusion.3), kind=kOutput, calls=%fused_computation.6 | convolution fusion | flops 2148532224 | bytes 8394752 | tf_op jit(solution)/shard_map/dot_general | solution.py:397
  13.6 0.0 copy-done.5
  13.7 0.0 copy-done.7
  13.7 2.3 compare_select_fusion.5
  16.0 0.0 copy-start.2
  16.0 0.0 copy-start
  16.0 0.3 slice_add_fusion
  16.4 0.8 pad_maximum_fusion
  17.2 0.0 all-reduce.2.cloned.1.call-update
  17.2 0.0 all-gather.2.cloned.1.call-start
  17.3 0.0 copy-done.2
  17.3 0.5 copy-done
  17.8 0.0 copy-start.3
  17.8 0.0 copy-start.4
  17.8 286.0 %shard_map.111 = (f32[512,2048]{1,0:T(8,128)}, f32[512,2048]{1,0:T(8,128)}, bf16[4,512,2048]{2,1,0:T(8,128)(2,1)}, bf16[4,512,2048]{2,1,0:T(8,128)(2,1)}) custom-call(bf16[512,2048]{1,0:T(8,128)(2,1)S(1)} %copy-done, bf16[512,2048]{1,0:T(8,128)(2,1)} %inp_ref.1, bf16[8192,2048]{1,0:T(8,128)(2,1)} %w_ref.1), custom_call_target="tpu_custom_call" | custom-call | flops 34359738368 | bytes 419430400 | tf_op jit(solution)/shard_map/pallas_call | solution.py:309
  303.8 0.0 copy-done.3
  303.8 0.0 copy-done.4
  303.8 0.1 select_reduce_fusion.1
  304.0 0.1 select_reduce_fusion
  304.1 0.3 compare_select_fusion.6
  304.4 0.0 all-reduce.2.cloned.1.call-done
  304.4 1.1 constant_dynamic-update-slice_fusion.15
  305.5 1.0 constant_dynamic-update-slice_fusion.7
  306.8 0.7 pad_maximum_fusion.1
  307.8 0.0 all-gather.2.cloned.1.call-update
  307.9 0.0 copy-start.6
  307.9 0.0 copy-start.8
  307.9 7.3 %select_convert_fusion.1 = bf16[512,2048]{1,0:T(8,128)(2,1)} fusion(f32[512,2048]{1,0:T(8,128)} %get-tuple-element.8, bf16[1024,2048]{1,0:T(8,128)(2,1)} %param.12, pred[512]{0:T(512)(128)(4,1)S(1)} %broadcast_compare_fusion, bf16[512,1024]{1,0:T(8,128)(2,1)S(1)} %constant_dynamic-update-slice_fusion, s32[1024]{0:T(1024)S(1)} %add_select_fusion, ...), kind=kOutput, calls=%fused_computation.13 | convolution fusion | flops 2151677952 | bytes 11540992 | tf_op jit(solution)/shard_map/dot_general | solution.py:416
  315.2 0.0 copy-done.6
  315.2 0.0 copy-done.8
  315.2 3.8 %select_convert_fusion = bf16[512,2048]{1,0:T(8,128)(2,1)} fusion(f32[512,2048]{1,0:T(8,128)S(1)} %copy-done.8, bf16[2048,1024]{1,0:T(8,128)(2,1)S(1)} %copy-done.6, pred[512]{0:T(512)(128)(4,1)S(1)} %broadcast_compare_fusion, bf16[512,1024]{1,0:T(8,128)(2,1)S(1)} %constant_dynamic-update-slice_fusion.8, s32[1024]{0:T(1024)S(1)} %add_select_fusion, ...), kind=kOutput, calls=%fused_computation.12 | convolution fusion | flops 2151677952 | bytes 11540992 | tf_op jit(solution)/shard_map/dot_general | solution.py:418
  319.0 5.6 %all-gather.2.cloned.1.call-done = bf16[2048,256]{1,0:T(8,128)(2,1)} async-done(((bf16[512,256]{1,0:T(8,128)(2,1)}), bf16[2048,256]{1,0:T(8,128)(2,1)}) %all-gather.2.cloned.1.call-update) | async-done | bytes 1048592 | tf_op jit(solution)/shard_map/all_gather | solution.py:410
  324.6 0.0 copy-start.1
  324.6 1.3 slice_dynamic-update-slice_fusion.6
  325.9 0.0 slice-start.2
  325.9 1.4 slice_dynamic-update-slice_fusion.5
  327.3 1.2 slice_dynamic-update-slice_fusion.4
  328.5 1.2 slice_dynamic-update-slice_fusion.3
  329.7 0.0 copy-done.1
  329.8 0.2 slice_dynamic-update-slice_fusion.2
  329.9 0.2 slice_dynamic-update-slice_fusion.1
  330.1 0.2 slice_dynamic-update-slice_fusion
  330.3 0.0 slice-start.3
  330.3 0.3 slice_dynamic-update-slice_fusion.7
  330.6 0.2 slice_dynamic-update-slice_fusion.13
  330.8 0.2 slice_dynamic-update-slice_fusion.12
  331.0 0.2 slice_dynamic-update-slice_fusion.11
  331.2 0.2 slice_dynamic-update-slice_fusion.10
  331.4 0.2 slice_dynamic-update-slice_fusion.9
  331.6 0.0 slice-start
  331.6 0.2 slice_dynamic-update-slice_fusion.8
  331.8 0.2 slice_dynamic-update-slice_fusion.15
  332.0 0.0 slice-done.2
  332.0 0.5 slice-done.3
  332.5 11.9 %multiply_bitcast_fusion.1 = f32[1,2048,1024]{2,1,0:T(8,128)} fusion(bf16[2048,2048]{1,0:T(8,128)(2,1)S(1)} %bitcast.24, bf16[2048,1024]{1,0:T(8,128)(2,1)S(1)} %slice_dynamic-update-slice_fusion.15, f32[1024]{0:T(1024)S(1)} %compare_select_fusion.12, s32[1024]{0:T(1024)S(1)} %add_select_fusion, s32[2048]{0:T(1024)S(1)} %bitcast.17), kind=kOutput, calls=%fused_computation.3 | convolution fusion | flops 8596226048 | bytes 20987904 | tf_op jit(solution)/shard_map/dot_general | solution.py:428
  344.4 0.0 slice-done
  344.4 0.0 slice-done.1
  344.4 12.1 %multiply_bitcast_fusion = f32[1,1024,2048]{2,1,0:T(8,128)} fusion(bf16[2048,2048]{1,0:T(8,128)(2,1)S(1)} %bitcast.21, bf16[2048,1024]{1,0:T(8,128)(2,1)S(1)} %get-tuple-element.19, f32[1024]{0:T(1024)S(1)} %compare_select_fusion.12, s32[1024]{0:T(1024)S(1)} %add_select_fusion, s32[2048]{0:T(1024)S(1)} %bitcast.18), kind=kOutput, calls=%fused_computation.2 | convolution fusion | flops 8596226048 | bytes 20987904 | tf_op jit(solution)/shard_map/dot_general | solution.py:429
  (25 shorter events, 0.6 us)
Async XLA Ops:
  7.2 297.2 %all-reduce.2.cloned.1.call-start = ((), (), s32[]{:S(2)}) async-start(), calls=%async_computation | async-start | bytes 1048576 | tf_op jit(solution)/shard_map/psum | solution.py:401
  8.3 5.4 %copy-start.5 = (bf16[2048,1024]{1,0:T(8,128)(2,1)S(1)}, bf16[2048,1024]{1,0:T(8,128)(2,1)}, u32[]{:S(2)}) copy-start(bf16[2048,1024]{1,0:T(8,128)(2,1)} %param.11) | copy-start | bytes 12582916
  8.3 5.4 %copy-start.7 = (bf16[512,2048]{1,0:T(8,128)(2,1)S(1)}, bf16[512,2048]{1,0:T(8,128)(2,1)}, u32[]{:S(2)}) copy-start(bf16[512,2048]{1,0:T(8,128)(2,1)} %inp_ref.1) | copy-start | bytes 6291460
  16.0 1.3 copy-start.2
  16.0 1.8 copy-start
  17.2 307.4 %all-gather.2.cloned.1.call-start = ((), (), s32[]{:S(2)}) async-start(), calls=%async_computation.1 | async-start | bytes 1310720 | tf_op jit(solution)/shard_map/all_gather | solution.py:410
  17.8 286.0 %copy-start.3 = (s32[16]{0:T(128)S(1)}, s32[16]{0:T(128)}, u32[]{:S(2)}) copy-start(s32[16]{0:T(128)} %param.15) | copy-start | bytes 196
  17.8 286.0 %copy-start.4 = (s32[16]{0:T(128)S(1)}, s32[16]{0:T(128)}, u32[]{:S(2)}) copy-start(s32[16]{0:T(128)} %param.14) | copy-start | bytes 196
  307.9 7.3 %copy-start.6 = (bf16[2048,1024]{1,0:T(8,128)(2,1)S(1)}, bf16[2048,1024]{1,0:T(8,128)(2,1)}, u32[]{:S(2)}) copy-start(bf16[2048,1024]{1,0:T(8,128)(2,1)} %param.11) | copy-start | bytes 12582916
  307.9 7.3 %copy-start.8 = (f32[512,2048]{1,0:T(8,128)S(1)}, f32[512,2048]{1,0:T(8,128)}, u32[]{:S(2)}) copy-start(f32[512,2048]{1,0:T(8,128)} %get-tuple-element.9) | copy-start | bytes 12582916
  324.6 5.1 %copy-start.1 = (bf16[2048,256]{1,0:T(8,128)(2,1)S(1)}, bf16[2048,256]{1,0:T(8,128)(2,1)}, u32[]{:S(2)}) copy-start(bf16[2048,256]{1,0:T(8,128)(2,1)} %all-gather.2.cloned.1.call-done) | copy-start | bytes 3145732
  325.9 6.1 %slice-start.2 = ((s8[8388608]{0:T(1024)(128)(4,1)}), s8[4194304]{0:T(1024)(128)(4,1)S(1)}, s32[]{:S(2)}) async-start(s8[8388608]{0:T(1024)(128)(4,1)} %bitcast.22), calls=%async_computation.4 | async-start | bytes 8388608
  330.3 2.2 slice-start.3
  331.6 12.8 %slice-start = ((s8[8388608]{0:T(1024)(128)(4,1)}), s8[4194304]{0:T(1024)(128)(4,1)S(1)}, s32[]{:S(2)}) async-start(s8[8388608]{0:T(1024)(128)(4,1)} %bitcast.19), calls=%async_computation.2 | async-start | bytes 8388608
  332.5 11.9 %slice-start.1 = ((s8[8388608]{0:T(1024)(128)(4,1)}), s8[4194304]{0:T(1024)(128)(4,1)S(1)}, s32[]{:S(2)}) async-start(s8[8388608]{0:T(1024)(128)(4,1)} %bitcast.19), calls=%async_computation.3 | async-start | bytes 8388608
Sparse Core Ops, SparseCore 0:
  17.3 53.0 all-reduce.1
  307.9 16.6 all-gather.1
